TPU v7x, 32 devices: a whole 2x2x4 slice. The times are simulated.
32 devices in a mesh: row: 4 (over y, core), col: 8 (over z, x).
Axes of the slice: x: 2, y: 2, z: 4, core: 2. Of those that a mesh axis runs over, the one named last changes fastest.
Arguments:
- positions: float32 [3, 512], P(None, ('row', 'col')), as said below
- thermal_noise: float32 [32, 3, 512], P(None, None, ('row', 'col')), as said below
Outputs:
- displacement: float32 [32, 3, 512], P(None, None, ('row', 'col'))
Inputs may be any that keep to these rules, and one draw needn't show every extreme that they name: `positions`: any two particles are at least 1.0 apart. `thermal_noise`: finite real entries.
All inputs are finite; a program needn't handle non-finite values.
Results may differ from a plain program's by a relative error of at most 0.0013.
Values may be sent and summed in bfloat16 or wider, within the bound.
A program may use at most 64 MiB of HBM per device.

v0:
```python
import jax
import jax.numpy as jnp
from jax import lax
from jax.sharding import PartitionSpec as P


def pair_tensor(rows_pos, cols_pos, retain):
    offsets = [rows_pos[a][None, :] - cols_pos[a][:, None] for a in range(3)]
    squared = offsets[0] * offsets[0] + offsets[1] * offsets[1] + offsets[2] * offsets[2]
    guarded = jnp.where(retain, squared, 4.0)
    inverse = lax.rsqrt(guarded)
    distance = guarded * inverse
    correlation = distance < 2.0
    inverse_cube = inverse * inverse * inverse
    inverse_fifth = inverse_cube * inverse * inverse
    isotropic = jnp.where(
        correlation, 1.0 - 0.28125 * distance, 0.75 * inverse + 0.5 * inverse_cube
    )
    dyadic = jnp.where(correlation, 0.09375 * inverse, 0.75 * inverse_cube - 1.5 * inverse_fifth)
    isotropic = jnp.where(retain, isotropic, 0.0)
    dyadic = jnp.where(retain, dyadic, 0.0)
    columns = []
    for b in range(3):
        elements = []
        for a in range(3):
            element = dyadic * offsets[a] * offsets[b]
            if a == b:
                element = element + isotropic
            elements.append(element)
        columns.append(jnp.stack(elements, axis=1))
    return jnp.stack(columns, axis=0)


def half_image(pos_rows, pos_cols, vec_rows, vec_cols, own_vector):
    row_devices = lax.axis_size("row")
    col_devices = lax.axis_size("col")
    row_index = lax.axis_index("row")
    col_index = lax.axis_index("col")
    samples = own_vector.shape[0]
    per_device = own_vector.shape[2]
    row_count = pos_rows.shape[1]
    row_label = row_index * col_devices * per_device + lax.iota(jnp.int32, row_count)
    group_size = min(row_devices, max(1, 128 // per_device))
    width = group_size * per_device
    group_count = row_devices // group_size
    sum_rows = jnp.zeros((samples, 3, row_count), jnp.float32)
    sum_cols = jnp.zeros((samples, 3, per_device * row_devices), jnp.float32)

    def add_group(group, totals):
        sum_rows, sum_cols = totals
        start = group * width
        cols_pos = lax.dynamic_slice_in_dim(pos_cols, start, width, 1)
        cols_vec = lax.dynamic_slice_in_dim(vec_cols, start, width, 2)
        local_cols = lax.iota(jnp.int32, width)
        segment = group * group_size + local_cols // per_device
        col_label = (segment * col_devices + col_index) * per_device + local_cols % per_device
        keep = segment >= row_index
        upper = (segment != row_index)[:, None] | (row_label[None, :] < col_label[:, None])
        retain = keep[:, None] & upper & (row_label[None, :] != col_label[:, None])
        tensor = pair_tensor(pos_rows, cols_pos, retain).astype(jnp.bfloat16)
        sum_rows = sum_rows + jnp.einsum(
            "kbj,bjai->kai", cols_vec, tensor, preferred_element_type=jnp.float32
        )
        credit = jnp.einsum("kai,bjai->kbj", vec_rows, tensor, preferred_element_type=jnp.float32)
        previous = lax.dynamic_slice_in_dim(sum_cols, start, width, 2)
        sum_cols = lax.dynamic_update_slice_in_dim(sum_cols, previous + credit, start, 2)
        return (sum_rows, sum_cols)

    totals = (sum_rows, sum_cols)
    totals = lax.fori_loop(row_index // group_size, group_count, add_group, totals)
    sum_rows, sum_cols = totals
    mobility_image = own_vector + lax.psum_scatter(sum_rows, "col", scatter_dimension=2, tiled=True)
    return mobility_image + lax.psum_scatter(sum_cols, "row", scatter_dimension=2, tiled=True)


def on_device(positions, thermal_noise):
    squares = lax.psum(jnp.sum(thermal_noise * thermal_noise, axis=(1, 2)), ("row", "col"))
    noise_length = jnp.sqrt(squares + 1e-06)
    basis_one = thermal_noise / noise_length[:, None, None]
    pos_cols, cols_one = (
        lax.all_gather(positions, "row", axis=1, tiled=True),
        lax.all_gather(basis_one, "row", axis=2, tiled=True),
    )
    pos_rows, rows_wide = (
        lax.all_gather(positions, "col", axis=1, tiled=True),
        lax.all_gather(basis_one, "col", axis=2, tiled=True),
    )
    image_one = half_image(
        pos_rows, pos_cols, rows_wide.astype(jnp.bfloat16), cols_one.astype(jnp.bfloat16), basis_one
    )
    alpha_one = lax.psum(jnp.sum(basis_one * image_one, axis=(1, 2)), ("row", "col"))
    remainder = image_one - alpha_one[:, None, None] * basis_one
    beta_squared = lax.psum(jnp.sum(remainder * remainder, axis=(1, 2)), ("row", "col"))
    beta_one = jnp.sqrt(beta_squared + 1e-06)
    basis_two = remainder / beta_one[:, None, None]
    narrow_two = basis_two.astype(jnp.bfloat16)
    cols_two = lax.all_gather(narrow_two, "row", axis=2, tiled=True)
    rows_two = lax.all_gather(narrow_two, "col", axis=2, tiled=True)
    image_two = half_image(pos_rows, pos_cols, rows_two, cols_two, basis_two)
    alpha_two = lax.psum(jnp.sum(basis_two * image_two, axis=(1, 2)), ("row", "col"))
    det_root = jnp.sqrt(alpha_one * alpha_two - beta_one * beta_one)
    trace_root = jnp.sqrt(alpha_one + alpha_two + 2.0 * det_root)
    weight_one = (alpha_one + det_root) / trace_root
    weight_two = beta_one / trace_root
    return (
        0.5
        * noise_length[:, None, None]
        * (weight_one[:, None, None] * basis_one + weight_two[:, None, None] * basis_two)
    )


def solution(mesh):
    return jax.shard_map(
        on_device,
        mesh=mesh,
        in_specs=(P(None, ("row", "col")), P(None, None, ("row", "col"))),
        out_specs=P(None, None, ("row", "col")),
        check_vma=False,
    )
```

profile of v0, /device:TPU:0, one launch (start us, length us, event | category | flops | bytes accessed | tf_op | source)
XLA Modules:
  0.0 451.7 jit_solution(3374881495807771110)
XLA Ops:
  6.5 0.0 reduce-scatter.7.cloned.1.call-start
  6.5 0.0 copy-start.3
  6.5 0.7 copy-done.3
  7.2 28.1 %all-gather = f32[8,16,3]{1,2,0:T(4,128)S(1)} all-gather(f32[1,16,3]{1,2,0:T(4,128)S(1)} %bitcast.133), channel_id=1, replica_groups=mesh['row'=4,'col'=8] {'col'}, dimensions={0}, use_global_device_ids=true | all-gather | bytes 1728 | tf_op jit(solution)/shard_map/all_gather | solution.py:85
  35.3 5.2 %all-gather.1 = f32[4,16,3]{1,2,0:T(4,128)S(1)} all-gather(f32[1,16,3]{1,2,0:T(4,128)S(1)} %bitcast.134), channel_id=1, replica_groups=mesh['row'=4,'col'=8] {'row'}, dimensions={0}, use_global_device_ids=true | all-gather | bytes 960 | tf_op jit(solution)/shard_map/all_gather | solution.py:81
  40.5 0.0 copy-done
  40.5 38.9 %psum.28 = f32[32]{0:T(128)S(1)} all-reduce(f32[32]{0:T(128)S(1)} %multiply_reduce_fusion.3), channel_id=1, replica_groups=mesh['row'=4,'col'=8] {'row','col'}, use_global_device_ids=true, to_apply=%region_1.0 | all-reduce | flops 32 | bytes 256 | tf_op jit(solution)/shard_map/psum | solution.py:77
  79.5 5.5 %all_gather.20 = bf16[32,3,64]{0,2,1:T(8,128)(2,1)S(1)} all-gather(bf16[32,3,16]{0,2,1:T(8,128)(2,1)S(1)} %convert.110), channel_id=1, replica_groups=mesh['row'=4,'col'=8] {'row'}, dimensions={2}, use_global_device_ids=true | all-gather | bytes 15360 | tf_op jit(solution)/shard_map/all_gather | solution.py:82
  85.0 0.1 copy.39
  85.1 30.6 %all_gather.21 = bf16[32,3,128]{0,2,1:T(8,128)(2,1)S(1)} all-gather(bf16[32,3,16]{0,2,1:T(8,128)(2,1)S(1)} %get-tuple-element.415), channel_id=1, replica_groups=mesh['row'=4,'col'=8] {'col'}, dimensions={2}, use_global_device_ids=true | all-gather | bytes 27648 | tf_op jit(solution)/shard_map/all_gather | solution.py:86
  115.6 0.1 copy.40
  115.7 0.1 reshape.5452
  115.8 0.1 reshape.5454
  115.9 0.7 while.30
  116.0 0.2 fusion.88
  116.3 0.2 fusion.90
  116.4 0.2 fusion.89
  116.6 0.7 copy.42
  117.4 0.0 reduce-scatter.7.cloned.1.call-update
  117.4 0.0 reduce-scatter.5.cloned.1.call-start
  117.5 0.8 copy.41
  118.3 0.0 reduce-scatter.5.cloned.1.call-update
  118.3 0.0 reduce-scatter.11.cloned.1.call-start
  118.3 17.6 %reduce-scatter.7.cloned.1.call-done = f32[32,3,16]{0,2,1:T(8,128)} async-done(((f32[32,3,64]{0,2,1:T(8,128)}), f32[32,3,16]{0,2,1:T(8,128)}) %reduce-scatter.7.cloned.1.call-update) | async-done | bytes 6160 | tf_op jit(solution)/shard_map/reduce_scatter | solution.py:73
  135.9 65.3 %reduce-scatter.5.cloned.1.call-done = f32[32,3,16]{0,2,1:T(8,128)} async-done(((f32[32,3,128]{0,2,1:T(8,128)}), f32[32,3,16]{0,2,1:T(8,128)}) %reduce-scatter.5.cloned.1.call-update) | async-done | bytes 6160 | tf_op jit(solution)/shard_map/reduce_scatter | solution.py:72
  201.2 0.8 multiply_reduce_fusion.2
  202.1 40.1 %psum.29 = f32[32]{0:T(128)S(1)} all-reduce(f32[32]{0:T(128)S(1)} %multiply_reduce_fusion.2), channel_id=1, replica_groups=mesh['row'=4,'col'=8] {'row','col'}, use_global_device_ids=true, to_apply=%region_7.8 | all-reduce | flops 32 | bytes 256 | tf_op jit(solution)/shard_map/psum | solution.py:91
  242.2 0.0 copy-done.1
  242.2 0.0 copy-done.2
  242.2 39.1 %psum.30 = f32[32]{0:T(128)S(1)} all-reduce(f32[32]{0:T(128)S(1)} %get-tuple-element.413), channel_id=1, replica_groups=mesh['row'=4,'col'=8] {'row','col'}, use_global_device_ids=true, to_apply=%region_9.10 | all-reduce | flops 32 | bytes 256 | tf_op jit(solution)/shard_map/psum | solution.py:93
  281.3 30.5 %all_gather.23 = bf16[32,3,128]{0,2,1:T(8,128)(2,1)S(1)} all-gather(bf16[32,3,16]{0,2,1:T(8,128)(2,1)S(1)} %fusion.71), channel_id=1, replica_groups=mesh['row'=4,'col'=8] {'col'}, dimensions={2}, use_global_device_ids=true | all-gather | bytes 27648 | tf_op jit(solution)/shard_map/all_gather | solution.py:98
  311.9 5.5 %all_gather.22 = bf16[32,3,64]{0,2,1:T(8,128)(2,1)S(1)} all-gather(bf16[32,3,16]{0,2,1:T(8,128)(2,1)S(1)} %fusion.71), channel_id=1, replica_groups=mesh['row'=4,'col'=8] {'row'}, dimensions={2}, use_global_device_ids=true | all-gather | bytes 15360 | tf_op jit(solution)/shard_map/all_gather | solution.py:97
  317.4 0.1 copy.44
  317.5 0.1 copy.43
  317.6 0.7 while.31
  317.7 0.2 fusion.94
  318.0 0.2 fusion.96
  318.2 0.2 fusion.95
  318.4 0.7 copy.46
  319.1 0.0 reduce-scatter.11.cloned.1.call-update
  319.1 0.0 reduce-scatter.9.cloned.1.call-start
  319.2 0.8 copy.45
  320.0 0.0 reduce-scatter.9.cloned.1.call-update
  320.0 18.4 %reduce-scatter.11.cloned.1.call-done = f32[32,3,16]{0,2,1:T(8,128)} async-done(((f32[32,3,64]{0,2,1:T(8,128)}), f32[32,3,16]{0,2,1:T(8,128)}) %reduce-scatter.11.cloned.1.call-update) | async-done | bytes 6160 | tf_op jit(solution)/shard_map/reduce_scatter | solution.py:73
  338.4 65.2 %reduce-scatter.9.cloned.1.call-done = f32[32,3,16]{0,2,1:T(8,128)} async-done(((f32[32,3,128]{0,2,1:T(8,128)}), f32[32,3,16]{0,2,1:T(8,128)}) %reduce-scatter.9.cloned.1.call-update) | async-done | bytes 6160 | tf_op jit(solution)/shard_map/reduce_scatter | solution.py:72
  403.6 0.8 multiply_reduce_fusion
  404.4 40.2 %psum.31 = f32[32]{0:T(128)S(1)} all-reduce(f32[32]{0:T(128)S(1)} %multiply_reduce_fusion), channel_id=1, replica_groups=mesh['row'=4,'col'=8] {'row','col'}, use_global_device_ids=true, to_apply=%region_15.16 | all-reduce | flops 32 | bytes 256 | tf_op jit(solution)/shard_map/psum | solution.py:100
  444.6 0.6 add_multiply_fusion
  (33 shorter events, 0.3 us)
Async XLA Ops:
  6.5 129.4 %reduce-scatter.7.cloned.1.call-start = ((), (), s32[]{:S(2)}) async-start(), calls=%async_computation.5 | async-start | bytes 122880 | tf_op jit(solution)/shard_map/reduce_scatter | solution.py:73
  6.5 0.7 copy-start.3
  7.2 33.2 %copy-start = (f32[32,3,16]{0,2,1:T(8,128)S(1)}, f32[32,3,16]{0,2,1:T(8,128)}, u32[]{:S(2)}) copy-start(f32[32,3,16]{0,2,1:T(8,128)} %param.7) | copy-start | bytes 18436
  117.4 83.8 %reduce-scatter.5.cloned.1.call-start = ((), (), s32[]{:S(2)}) async-start(), calls=%async_computation.4 | async-start | bytes 221184 | tf_op jit(solution)/shard_map/reduce_scatter | solution.py:72
  118.3 220.2 %reduce-scatter.11.cloned.1.call-start = ((), (), s32[]{:S(2)}) async-start(), calls=%async_computation.7 | async-start | bytes 122880 | tf_op jit(solution)/shard_map/reduce_scatter | solution.py:73
  135.9 106.2 %copy-start.1 = (f32[32,3,16]{0,2,1:T(8,128)S(1)}, f32[32,3,16]{0,2,1:T(8,128)}, u32[]{:S(2)}) copy-start(f32[32,3,16]{0,2,1:T(8,128)} %reduce-scatter.7.cloned.1.call-done) | copy-start | bytes 18436
  201.2 40.9 %copy-start.2 = (f32[32,3,16]{0,2,1:T(8,128)S(1)}, f32[32,3,16]{0,2,1:T(8,128)}, u32[]{:S(2)}) copy-start(f32[32,3,16]{0,2,1:T(8,128)} %reduce-scatter.5.cloned.1.call-done) | copy-start | bytes 18436
  319.1 84.5 %reduce-scatter.9.cloned.1.call-start = ((), (), s32[]{:S(2)}) async-start(), calls=%async_computation.6 | async-start | bytes 221184 | tf_op jit(solution)/shard_map/reduce_scatter | solution.py:72
Sparse Core Ops, SparseCore 0:
  117.5 18.3 reduce-scatter.6
  139.2 61.9 reduce-scatter.4
  319.2 19.1 reduce-scatter.10
  341.6 61.9 reduce-scatter.8
where the time goes:
time: 453 us; the launch traced here: 452 us
  blocking collectives  264 us (58%)
  waiting for transfers between devices  167 us (37%)
  between operations  13.2 us (3%)
    reduce_scatter x2, waiting for transfers between devices, half_image(): lax.psum_scatter(sum_rows, 'col', scatter_dimension=2, tiled=True)  130 us
    psum x1, blocking collectives, on_device(): lax.psum(jnp.sum(basis_two * image_two, axis=(1, 2)), ('row', 'col'))  40.2 us
    psum x1, blocking collectives, on_device(): lax.psum(jnp.sum(basis_one * image_one, axis=(1, 2)), ('row', 'col'))  40.1 us
    psum x1, blocking collectives, on_device(): lax.psum(jnp.sum(remainder * remainder, axis=(1, 2)), ('row', 'col'))  39.1 us
    psum x1, blocking collectives, on_device(): lax.psum(jnp.sum(thermal_noise * thermal_noise, axis=(1, 2)), ('row', 'co...  38.9 us
    reduce_scatter x2, waiting for transfers between devices, half_image(): lax.psum_scatter(sum_cols, 'row', scatter_dimension=2, tiled=True)  36 us
    all_gather x1, blocking collectives, on_device(): lax.all_gather(basis_one, 'col', axis=2, tiled=True)  30.6 us
    all_gather x1, blocking collectives, on_device(): rows_two = lax.all_gather(narrow_two, 'col', axis=2, tiled=True)  30.5 us
  transfers between devices with their start and end apart: 4, of which 4 were waited for; matrix products, arithmetic and copies ran while one was open for 0% of the time, Pallas kernels for 0%

commit v1 on v0

--- a/solution.py
+++ b/solution.py
@@ -97,7 +97,7 @@
     cols_two = lax.all_gather(narrow_two, "row", axis=2, tiled=True)
     rows_two = lax.all_gather(narrow_two, "col", axis=2, tiled=True)
     image_two = half_image(pos_rows, pos_cols, rows_two, cols_two, basis_two)
-    alpha_two = lax.psum(jnp.sum(basis_two * image_two, axis=(1, 2)), ("row", "col"))
+    alpha_two = lax.psum(lax.psum(jnp.sum(basis_two * image_two, axis=(1, 2)), "col"), "row")
     det_root = jnp.sqrt(alpha_one * alpha_two - beta_one * beta_one)
     trace_root = jnp.sqrt(alpha_one + alpha_two + 2.0 * det_root)
     weight_one = (alpha_one + det_root) / trace_root

time: 453 us -> 437 us (0.965)
  blocking collectives: 264 us -> 249 us
    psum x1 -> x2, blocking collectives: 40.2 us -> 25.1 us  [the longest x1 19.5 us: on_device(): lax.psum(jnp.sum(basis_two * image_two, axis=(1, 2)), 'col')]
where the time goes in v1:
time: 437 us
  blocking collectives  249 us (57%)
  waiting for transfers between devices  167 us (38%)
  between operations  13.2 us (3%)
    reduce_scatter x2, waiting for transfers between devices, half_image(): lax.psum_scatter(sum_rows, 'col', scatter_dimension=2, tiled=True)  130 us
    psum x1, blocking collectives, on_device(): lax.psum(jnp.sum(basis_one * image_one, axis=(1, 2)), ('row', 'col'))  40.1 us
    psum x1, blocking collectives, on_device(): lax.psum(jnp.sum(remainder * remainder, axis=(1, 2)), ('row', 'col'))  39.1 us
    psum x1, blocking collectives, on_device(): lax.psum(jnp.sum(thermal_noise * thermal_noise, axis=(1, 2)), ('row', 'co...  38.9 us
    reduce_scatter x2, waiting for transfers between devices, half_image(): lax.psum_scatter(sum_cols, 'row', scatter_dimension=2, tiled=True)  36 us
    all_gather x1, blocking collectives, on_device(): lax.all_gather(basis_one, 'col', axis=2, tiled=True)  30.6 us
    all_gather x1, blocking collectives, on_device(): rows_two = lax.all_gather(narrow_two, 'col', axis=2, tiled=True)  30.5 us
    all_gather x1, blocking collectives, on_device(): lax.all_gather(positions, 'col', axis=1, tiled=True)  28.1 us
  transfers between devices with their start and end apart: 4, of which 4 were waited for; matrix products, arithmetic and copies ran while one was open for 0% of the time, Pallas kernels for 0%

profile of v1, /device:TPU:0, one launch (start us, length us, event | category | flops | bytes accessed | tf_op | source)
XLA Modules:
  0.0 436.7 jit_solution(14192137315507088966)
XLA Ops:
  6.5 0.0 reduce-scatter.7.cloned.1.call-start
  6.5 0.7 copy-done.3
  7.2 28.1 %all-gather = f32[8,16,3]{1,2,0:T(4,128)S(1)} all-gather(f32[1,16,3]{1,2,0:T(4,128)S(1)} %bitcast.133), channel_id=1, replica_groups=mesh['row'=4,'col'=8] {'col'}, dimensions={0}, use_global_device_ids=true | all-gather | bytes 1728 | tf_op jit(solution)/shard_map/all_gather | solution.py:85
  35.3 5.2 %all-gather.1 = f32[4,16,3]{1,2,0:T(4,128)S(1)} all-gather(f32[1,16,3]{1,2,0:T(4,128)S(1)} %bitcast.134), channel_id=1, replica_groups=mesh['row'=4,'col'=8] {'row'}, dimensions={0}, use_global_device_ids=true | all-gather | bytes 960 | tf_op jit(solution)/shard_map/all_gather | solution.py:81
  40.5 0.0 copy-done
  40.5 38.9 %psum.35 = f32[32]{0:T(128)S(1)} all-reduce(f32[32]{0:T(128)S(1)} %multiply_reduce_fusion.3), channel_id=1, replica_groups=mesh['row'=4,'col'=8] {'row','col'}, use_global_device_ids=true, to_apply=%region_1.0 | all-reduce | flops 32 | bytes 256 | tf_op jit(solution)/shard_map/psum | solution.py:77
  79.5 5.5 %all_gather.20 = bf16[32,3,64]{0,2,1:T(8,128)(2,1)S(1)} all-gather(bf16[32,3,16]{0,2,1:T(8,128)(2,1)S(1)} %convert.110), channel_id=1, replica_groups=mesh['row'=4,'col'=8] {'row'}, dimensions={2}, use_global_device_ids=true | all-gather | bytes 15360 | tf_op jit(solution)/shard_map/all_gather | solution.py:82
  85.0 0.1 copy.39
  85.1 30.6 %all_gather.21 = bf16[32,3,128]{0,2,1:T(8,128)(2,1)S(1)} all-gather(bf16[32,3,16]{0,2,1:T(8,128)(2,1)S(1)} %get-tuple-element.415), channel_id=1, replica_groups=mesh['row'=4,'col'=8] {'col'}, dimensions={2}, use_global_device_ids=true | all-gather | bytes 27648 | tf_op jit(solution)/shard_map/all_gather | solution.py:86
  115.6 0.1 copy.40
  115.7 0.1 reshape.5452
  115.8 0.1 reshape.5454
  115.9 0.7 while.30
  116.0 0.2 fusion.88
  116.3 0.2 fusion.90
  116.4 0.2 fusion.89
  116.6 0.7 copy.42
  117.4 0.0 reduce-scatter.7.cloned.1.call-update
  117.4 0.0 reduce-scatter.5.cloned.1.call-start
  117.5 0.8 copy.41
  118.3 0.0 reduce-scatter.5.cloned.1.call-update
  118.3 0.0 reduce-scatter.11.cloned.1.call-start
  118.3 17.6 %reduce-scatter.7.cloned.1.call-done = f32[32,3,16]{0,2,1:T(8,128)} async-done(((f32[32,3,64]{0,2,1:T(8,128)}), f32[32,3,16]{0,2,1:T(8,128)}) %reduce-scatter.7.cloned.1.call-update) | async-done | bytes 6160 | tf_op jit(solution)/shard_map/reduce_scatter | solution.py:73
  135.9 65.3 %reduce-scatter.5.cloned.1.call-done = f32[32,3,16]{0,2,1:T(8,128)} async-done(((f32[32,3,128]{0,2,1:T(8,128)}), f32[32,3,16]{0,2,1:T(8,128)}) %reduce-scatter.5.cloned.1.call-update) | async-done | bytes 6160 | tf_op jit(solution)/shard_map/reduce_scatter | solution.py:72
  201.2 0.8 multiply_reduce_fusion.2
  202.1 40.1 %psum.36 = f32[32]{0:T(128)S(1)} all-reduce(f32[32]{0:T(128)S(1)} %multiply_reduce_fusion.2), channel_id=1, replica_groups=mesh['row'=4,'col'=8] {'row','col'}, use_global_device_ids=true, to_apply=%region_7.8 | all-reduce | flops 32 | bytes 256 | tf_op jit(solution)/shard_map/psum | solution.py:91
  242.2 0.0 copy-done.1
  242.2 0.0 copy-done.2
  242.2 39.1 %psum.37 = f32[32]{0:T(128)S(1)} all-reduce(f32[32]{0:T(128)S(1)} %get-tuple-element.413), channel_id=1, replica_groups=mesh['row'=4,'col'=8] {'row','col'}, use_global_device_ids=true, to_apply=%region_9.10 | all-reduce | flops 32 | bytes 256 | tf_op jit(solution)/shard_map/psum | solution.py:93
  281.3 30.5 %all_gather.23 = bf16[32,3,128]{0,2,1:T(8,128)(2,1)S(1)} all-gather(bf16[32,3,16]{0,2,1:T(8,128)(2,1)S(1)} %fusion.71), channel_id=1, replica_groups=mesh['row'=4,'col'=8] {'col'}, dimensions={2}, use_global_device_ids=true | all-gather | bytes 27648 | tf_op jit(solution)/shard_map/all_gather | solution.py:98
  311.9 5.5 %all_gather.22 = bf16[32,3,64]{0,2,1:T(8,128)(2,1)S(1)} all-gather(bf16[32,3,16]{0,2,1:T(8,128)(2,1)S(1)} %fusion.71), channel_id=1, replica_groups=mesh['row'=4,'col'=8] {'row'}, dimensions={2}, use_global_device_ids=true | all-gather | bytes 15360 | tf_op jit(solution)/shard_map/all_gather | solution.py:97
  317.4 0.1 copy.44
  317.5 0.1 copy.43
  317.6 0.7 while.31
  317.7 0.2 fusion.94
  318.0 0.2 fusion.96
  318.2 0.2 fusion.95
  318.4 0.7 copy.46
  319.1 0.0 reduce-scatter.11.cloned.1.call-update
  319.1 0.0 reduce-scatter.9.cloned.1.call-start
  319.2 0.8 copy.45
  320.0 0.0 reduce-scatter.9.cloned.1.call-update
  320.0 18.4 %reduce-scatter.11.cloned.1.call-done = f32[32,3,16]{0,2,1:T(8,128)} async-done(((f32[32,3,64]{0,2,1:T(8,128)}), f32[32,3,16]{0,2,1:T(8,128)}) %reduce-scatter.11.cloned.1.call-update) | async-done | bytes 6160 | tf_op jit(solution)/shard_map/reduce_scatter | solution.py:73
  338.4 65.2 %reduce-scatter.9.cloned.1.call-done = f32[32,3,16]{0,2,1:T(8,128)} async-done(((f32[32,3,128]{0,2,1:T(8,128)}), f32[32,3,16]{0,2,1:T(8,128)}) %reduce-scatter.9.cloned.1.call-update) | async-done | bytes 6160 | tf_op jit(solution)/shard_map/reduce_scatter | solution.py:72
  403.6 0.8 multiply_reduce_fusion
  404.4 19.5 %psum.38 = f32[32]{0:T(128)S(1)} all-reduce(f32[32]{0:T(128)S(1)} %multiply_reduce_fusion), channel_id=1, replica_groups=mesh['row'=4,'col'=8] {'col'}, use_global_device_ids=true, to_apply=%region_15.16 | all-reduce | flops 32 | bytes 256 | tf_op jit(solution)/shard_map/psum | solution.py:100
  423.8 5.6 %psum.39 = f32[32]{0:T(128)S(1)} all-reduce(f32[32]{0:T(128)S(1)} %psum.38), channel_id=1, replica_groups=mesh['row'=4,'col'=8] {'row'}, use_global_device_ids=true, to_apply=%region_16.17 | all-reduce | flops 32 | bytes 256 | tf_op jit(solution)/shard_map/psum | solution.py:100
  429.5 0.6 add_multiply_fusion
  (34 shorter events, 0.3 us)
Async XLA Ops:
  6.5 129.4 %reduce-scatter.7.cloned.1.call-start = ((), (), s32[]{:S(2)}) async-start(), calls=%async_computation.5 | async-start | bytes 122880 | tf_op jit(solution)/shard_map/reduce_scatter | solution.py:73
  6.5 0.7 copy-start.3
  7.2 33.2 %copy-start = (f32[32,3,16]{0,2,1:T(8,128)S(1)}, f32[32,3,16]{0,2,1:T(8,128)}, u32[]{:S(2)}) copy-start(f32[32,3,16]{0,2,1:T(8,128)} %param.7) | copy-start | bytes 18436
  117.4 83.8 %reduce-scatter.5.cloned.1.call-start = ((), (), s32[]{:S(2)}) async-start(), calls=%async_computation.4 | async-start | bytes 221184 | tf_op jit(solution)/shard_map/reduce_scatter | solution.py:72
  118.3 220.2 %reduce-scatter.11.cloned.1.call-start = ((), (), s32[]{:S(2)}) async-start(), calls=%async_computation.7 | async-start | bytes 122880 | tf_op jit(solution)/shard_map/reduce_scatter | solution.py:73
  135.9 106.2 %copy-start.1 = (f32[32,3,16]{0,2,1:T(8,128)S(1)}, f32[32,3,16]{0,2,1:T(8,128)}, u32[]{:S(2)}) copy-start(f32[32,3,16]{0,2,1:T(8,128)} %reduce-scatter.7.cloned.1.call-done) | copy-start | bytes 18436
  201.2 40.9 %copy-start.2 = (f32[32,3,16]{0,2,1:T(8,128)S(1)}, f32[32,3,16]{0,2,1:T(8,128)}, u32[]{:S(2)}) copy-start(f32[32,3,16]{0,2,1:T(8,128)} %reduce-scatter.5.cloned.1.call-done) | copy-start | bytes 18436
  319.1 84.5 %reduce-scatter.9.cloned.1.call-start = ((), (), s32[]{:S(2)}) async-start(), calls=%async_computation.6 | async-start | bytes 221184 | tf_op jit(solution)/shard_map/reduce_scatter | solution.py:72
Sparse Core Ops, SparseCore 0:
  117.5 18.3 reduce-scatter.6
  139.2 61.9 reduce-scatter.4
  319.2 19.1 reduce-scatter.10
  341.6 61.9 reduce-scatter.8
